TPU v7x, 32 devices: a whole 2x2x4 slice. The times are simulated.
32 devices in a mesh: groups: 2 (over y), ulysses: 8 (over z, x), seq: 2 (over core).
Axes of the slice: x: 2, y: 2, z: 4, core: 2. Of those that a mesh axis runs over, the one named last changes fastest.
Arguments:
- query_states: bfloat16 [2048, 8192], P(('groups', 'ulysses', 'seq')), parts along dimension 0, may hold values from -6 to 6
- key_states: bfloat16 [2048, 1024], P(('groups', 'ulysses', 'seq')), parts along dimension 0, may hold values from -6 to 6
- value_states: bfloat16 [2048, 1024], P(('groups', 'ulysses', 'seq')), parts along dimension 0, may hold values from -6 to 6
- turn_ids: int32 [2048], P('groups'), parts along dimension 0, may hold values from 0 to 3, never falling along the last dimension, each value on 1 to 512 neighbouring positions
- judge_positions: int32 [256], P('groups'), parts along dimension 0, may hold values from 0 to 1023, as said below
Outputs:
- attended_states: bfloat16 [2048, 8192], P(('groups', 'ulysses', 'seq')), parts along dimension 0
There are 2 independent parts, one for each index of `groups`. A program takes and returns all parts, laid end to end along the dimension named above; each array names one. Nothing has to cross between parts.
Inputs may be any that keep to these rules, and one draw needn't show every extreme that they name: `turn_ids`: turn numbers never fall along the conversation; every turn spans 1 to 512 tokens, one exactly that many. `judge_positions`: distinct positions, 0 and 1023 among them.
All inputs are finite; a program needn't handle non-finite values.
Results may differ from a plain program's by a relative error of at most 0.004.
Values may be sent and summed in bfloat16 or wider, within the bound.
No kernel may reach another device: no remote copies, remote signals or barrier semaphores. Data moves between devices by JAX's collectives and lax.ppermute only.
A program may use at most 64 MiB of HBM per device.

v0:
```python
import math
import jax
import jax.numpy as jnp
from jax import lax
from jax.sharding import PartitionSpec as P

HEAD_DIM = 128
floor_score = -1e30


def absorb(
    carried,
    query_block,
    query_place,
    query_turn,
    keys_block,
    values_block,
    keys_place,
    keys_turn,
    keys_judge,
    scaling,
):
    maxima, totals, running = carried
    scores = (
        jnp.einsum("qhd,kd->qhk", query_block, keys_block, preferred_element_type=jnp.float32)
        * scaling
    )
    visible = (keys_place[None, :] <= query_place[:, None]) & (
        (keys_turn[None, :] == query_turn[:, None]) | keys_judge[None, :]
    )
    scores = jnp.where(visible[:, None, :], scores, floor_score)
    newest = jnp.maximum(maxima, jnp.max(scores, axis=2))
    factor = jnp.exp(maxima - newest)
    weights = jnp.exp(scores - newest[:, :, None])
    totals = totals * factor + jnp.sum(weights, axis=2)
    running = running * factor[:, :, None] + jnp.einsum(
        "qhk,kd->qhd",
        weights.astype(jnp.bfloat16),
        values_block,
        preferred_element_type=jnp.float32,
    )
    return (newest, totals, running)


def attend(
    carried,
    queries,
    query_place,
    query_turn,
    key_rows,
    value_rows,
    keys_place,
    keys_turn,
    keys_judge,
    scaling,
):
    query_count = queries.shape[0]
    key_count = key_rows.shape[0]
    query_step = math.gcd(query_count, 512)
    key_step = math.gcd(key_count, 512)

    def over_queries(row_index, totals_all):
        offset = row_index * query_step
        query_block = lax.dynamic_slice_in_dim(queries, offset, query_step, 0)
        block_place = lax.dynamic_slice_in_dim(query_place, offset, query_step, 0)
        block_turn = lax.dynamic_slice_in_dim(query_turn, offset, query_step, 0)
        window = tuple(
            (lax.dynamic_slice_in_dim(member, offset, query_step, 0) for member in totals_all)
        )

        def over_keys(key_index, current):
            key_offset = key_index * key_step
            keys_block = lax.dynamic_slice_in_dim(key_rows, key_offset, key_step, 0)
            values_block = lax.dynamic_slice_in_dim(value_rows, key_offset, key_step, 0)
            block_keys_place = lax.dynamic_slice_in_dim(keys_place, key_offset, key_step, 0)
            block_keys_turn = lax.dynamic_slice_in_dim(keys_turn, key_offset, key_step, 0)
            block_keys_judge = lax.dynamic_slice_in_dim(keys_judge, key_offset, key_step, 0)
            return lax.cond(
                jnp.max(block_place) >= jnp.min(block_keys_place),
                lambda inside: absorb(
                    inside,
                    query_block,
                    block_place,
                    block_turn,
                    keys_block,
                    values_block,
                    block_keys_place,
                    block_keys_turn,
                    block_keys_judge,
                    scaling,
                ),
                lambda inside: inside,
                current,
            )

        window = lax.fori_loop(0, key_count // key_step, over_keys, window)
        return tuple(
            (
                lax.dynamic_update_slice_in_dim(member, updated, offset, 0)
                for member, updated in zip(totals_all, window)
            )
        )

    return lax.fori_loop(0, query_count // query_step, over_queries, carried)


def spread(array, copies):
    row_count = array.shape[0]
    shared_heads = array.shape[1] // HEAD_DIM
    widened = jnp.broadcast_to(
        array.reshape(row_count, shared_heads, 1, HEAD_DIM),
        (row_count, shared_heads, copies // shared_heads, HEAD_DIM),
    )
    return widened.reshape(row_count, copies, HEAD_DIM)


def shards(query_states, key_states, value_states, turn_ids, judge_positions):
    tokens_here = query_states.shape[0]
    ulysses_count = lax.axis_size("ulysses")
    stripe_count = lax.axis_size("seq")
    stripe = lax.axis_index("seq")
    heads_here = query_states.shape[1] // HEAD_DIM // ulysses_count
    seq_total = tokens_here * ulysses_count * stripe_count
    scaling = 1.0 / math.sqrt(HEAD_DIM)
    positions = jnp.arange(seq_total, dtype=jnp.int32)
    judged = jnp.any(positions[:, None] == judge_positions[None, :], axis=1)
    exchanged = lax.all_to_all(
        query_states.reshape(tokens_here, ulysses_count, heads_here * HEAD_DIM),
        "ulysses",
        split_axis=1,
        concat_axis=0,
        tiled=True,
    )
    query_total = ulysses_count * tokens_here
    queries = exchanged.reshape(query_total, heads_here, HEAD_DIM)
    local_rows = jnp.arange(query_total, dtype=jnp.int32)
    query_place = (
        local_rows // tokens_here * stripe_count + stripe
    ) * tokens_here + local_rows % tokens_here
    query_turn = jnp.take(turn_ids, query_place)
    carried = (
        jnp.full((query_total, heads_here), floor_score, jnp.float32),
        jnp.zeros((query_total, heads_here), jnp.float32),
        jnp.zeros((query_total, heads_here, HEAD_DIM), jnp.float32),
    )
    keys_out, values_out = (
        lax.all_to_all(
            spread(key_states, ulysses_count), "ulysses", split_axis=1, concat_axis=0, tiled=True
        ),
        lax.all_to_all(
            spread(value_states, ulysses_count), "ulysses", split_axis=1, concat_axis=0, tiled=True
        ),
    )
    key_rows = keys_out.reshape(query_total, HEAD_DIM)
    value_rows = values_out.reshape(query_total, HEAD_DIM)
    pieces = (
        lax.all_gather(key_rows, "seq", axis=0, tiled=True),
        lax.all_gather(value_rows, "seq", axis=0, tiled=True),
    )
    piece_rows = pieces[0].shape[0]
    gathered_rows = jnp.arange(piece_rows, dtype=jnp.int32)
    source_stripe = gathered_rows // query_total
    within = gathered_rows % query_total
    key_place = (
        within // tokens_here * stripe_count + source_stripe
    ) * tokens_here + within % tokens_here
    maxima, totals, running = attend(
        carried,
        queries,
        query_place,
        query_turn,
        pieces[0],
        pieces[1],
        key_place,
        jnp.take(turn_ids, key_place),
        jnp.take(judged, key_place),
        scaling,
    )
    result = (
        (running / totals[:, :, None])
        .astype(jnp.bfloat16)
        .reshape(query_total, 1, heads_here * HEAD_DIM)
    )
    returned = lax.all_to_all(result, "ulysses", split_axis=0, concat_axis=1, tiled=True)
    return returned.reshape(tokens_here, ulysses_count * heads_here * HEAD_DIM)


def solution(mesh):
    placed = (
        P(("groups", "ulysses", "seq"), None),
        P(("groups", "ulysses", "seq"), None),
        P(("groups", "ulysses", "seq"), None),
        P("groups"),
        P("groups"),
    )
    return jax.shard_map(
        shards,
        mesh=mesh,
        in_specs=placed,
        out_specs=P(("groups", "ulysses", "seq"), None),
        check_vma=False,
    )
```

profile of v0, /device:TPU:0, one launch (start us, length us, event | category | flops | bytes accessed | tf_op | source)
XLA Modules:
  0.0 126.2 jit_solution(8405274671733121284)
XLA Ops:
  1.6 7.3 %all-to-all-start = ((bf16[64,8,128]{2,0,1:T(8,128)(2,1)}), bf16[64,8,128]{2,0,1:T(8,128)(2,1)S(1)}, u32[]{:S(2)}, u32[]{:S(2)}) async-start(bf16[64,8,128]{2,0,1:T(8,128)(2,1)} %copy_bitcast_fusion.2), calls=%async_computation | async-start | bytes 262144 | tf_op jit(solution)/shard_map/all_to_all | solution.py:147
  8.9 1.6 %copy_bitcast_fusion.1 = bf16[64,8,128]{2,0,1:T(8,128)(2,1)} fusion(bf16[64,1024]{1,0:T(8,128)(2,1)} %param.11), kind=kLoop, calls=%fused_computation.40 | loop fusion | bytes 262144 | tf_op jit(solution)/shard_map/reshape;reshape | solution.py:114
  10.4 5.8 %all-to-all-done = bf16[64,8,128]{2,0,1:T(8,128)(2,1)S(1)} async-done(((bf16[64,8,128]{2,0,1:T(8,128)(2,1)}), bf16[64,8,128]{2,0,1:T(8,128)(2,1)S(1)}, u32[]{:S(2)}, u32[]{:S(2)}) %all-to-all-start) | async-done | bytes 131104 | tf_op jit(solution)/shard_map/all_to_all | solution.py:147
  16.2 3.4 %all-to-all-start.2 = ((bf16[64,8,128]{2,0,1:T(8,128)(2,1)}), bf16[64,8,128]{2,0,1:T(8,128)(2,1)S(1)}, u32[]{:S(2)}, u32[]{:S(2)}) async-start(bf16[64,8,128]{2,0,1:T(8,128)(2,1)} %copy_bitcast_fusion.1), calls=%async_computation.2 | async-start | bytes 262144 | tf_op jit(solution)/shard_map/all_to_all | solution.py:150
  19.6 2.3 %copy.51 = bf16[8,8,8,1024]{3,2,0,1:T(8,128)(2,1)} copy(bf16[8,8,8,1024]{3,2,1,0:T(8,128)(2,1)} %bitcast.71) | data formatting | bytes 2097152 | tf_op jit(solution)/shard_map/reshape | solution.py:128
  21.9 5.0 %all-to-all-done.2 = bf16[64,8,128]{2,0,1:T(8,128)(2,1)S(1)} async-done(((bf16[64,8,128]{2,0,1:T(8,128)(2,1)}), bf16[64,8,128]{2,0,1:T(8,128)(2,1)S(1)}, u32[]{:S(2)}, u32[]{:S(2)}) %all-to-all-start.2) | async-done | bytes 131104 | tf_op jit(solution)/shard_map/all_to_all | solution.py:150
  26.9 3.6 %all-to-all-start.1 = ((bf16[64,8,1024]{2,0,1:T(8,128)(2,1)}), bf16[64,8,1024]{2,0,1:T(8,128)(2,1)S(1)}, u32[]{:S(2)}, u32[]{:S(2)}) async-start(bf16[64,8,1024]{2,0,1:T(8,128)(2,1)} %bitcast.66), calls=%async_computation.1 | async-start | bytes 2097152 | tf_op jit(solution)/shard_map/all_to_all | solution.py:127
  30.5 5.7 %gather_fusion = s32[1024]{0:T(1024)S(1)} fusion(s32[1024]{0:T(1024)} %param.12, s32[1024]{0:T(1024)S(1)} %broadcast_clamp_fusion), kind=kCustom, calls=%fused_computation | custom fusion | bytes 12288 | tf_op jit(solution)/shard_map/jit(_take)/gather | solution.py:175
  36.3 2.3 %gather_fusion.1 = s32[512]{0:T(512)S(1)} fusion(s32[1024]{0:T(1024)S(1)} %copy-done.1, s32[1024]{0:T(1024)S(1)} %pad_clamp_fusion), kind=kCustom, calls=%fused_computation.1 | custom fusion | bytes 6144 | tf_op jit(solution)/shard_map/jit(_take)/gather | solution.py:140
  38.8 6.8 %gather_fusion.2 = pred[1024]{0:T(1024)(128)(4,1)S(1)} fusion(pred[1024]{0:T(1024)(128)(4,1)S(1)} %fusion.24, s32[1024]{0:T(1024)S(1)} %broadcast_clamp_fusion), kind=kCustom, calls=%fused_computation.2 | custom fusion | bytes 6144 | tf_op jit(solution)/shard_map/jit(_take)/gather | solution.py:176
  46.2 1.3 %and_select_fusion.6 = (s32[512]{0:T(512)}, s32[]{:T(128)}) fusion(s32[512]{0:T(512)S(1)} %gather_fusion.1, s32[]{:T(128)} %axis_index.12), kind=kLoop, calls=%fused_computation.115 | loop fusion | flops 12287 | bytes 4104 | tf_op jit(solution)/shard_map/jit(_take)/select_n | solution.py:140
  48.1 2.0 %all_gather.6 = bf16[1024,128]{1,0:T(8,128)(2,1)S(1)} all-gather(bf16[512,128]{1,0:T(8,128)(2,1)S(1)} %bitcast.72), channel_id=1, replica_groups=mesh['groups'=2,'ulysses'=8,'seq'=2] {'seq'}, dimensions={0}, use_global_device_ids=true | all-gather | bytes 393216 | tf_op jit(solution)/shard_map/all_gather | solution.py:157
  50.1 2.1 %all_gather.7 = bf16[1024,128]{1,0:T(8,128)(2,1)} all-gather(bf16[512,128]{1,0:T(8,128)(2,1)S(1)} %bitcast.73), channel_id=1, replica_groups=mesh['groups'=2,'ulysses'=8,'seq'=2] {'seq'}, dimensions={0}, use_global_device_ids=true | all-gather | bytes 393216 | tf_op jit(solution)/shard_map/all_gather | solution.py:158
  52.2 1.9 %all-to-all-done.1 = bf16[64,8,1024]{2,0,1:T(8,128)(2,1)S(1)} async-done(((bf16[64,8,1024]{2,0,1:T(8,128)(2,1)}), bf16[64,8,1024]{2,0,1:T(8,128)(2,1)S(1)}, u32[]{:S(2)}, u32[]{:S(2)}) %all-to-all-start.1) | async-done | bytes 1048608 | tf_op jit(solution)/shard_map/all_to_all | solution.py:127
  55.2 31.6 %while.31 = (s32[]{:T(128)}, f32[512,8]{0,1:T(8,128)S(1)}, f32[512,8]{0,1:T(8,128)}, f32[512,8,128]{2,0,1:T(8,128)S(1)}, s32[1024]{0:T(1024)}, /*index=5*/s32[]{...) while((s32[]{:T(128)}, f32[512,8]{0,1:T(8,128)S(1)}, ...), condition=%wide.region_8.9_spmd.clone, body=%wide.region_2.8_spmd.clone.sunk | while | flops 1098925056 | bytes 33209420 | solution.py:96
  55.2 2.0 %fusion.67 = (s32[]{:T(128)}, s32[512]{0:T(512)}) fusion(s32[1024]{0:T(1024)} %get-tuple-element.768, s32[]{:T(128)} %select_n.391), kind=kLoop, calls=%fused_computation.117.clone.1 | loop fusion | flops 511 | bytes 4104 | tf_op jit(solution)/shard_map/while/body/eval_jaxpr/while/body/eval_jaxpr/reduce_min | solution.py:79
  61.5 9.5 %conditional.3 = ((f32[512,8]{0,1:T(8,128)S(1)}, f32[512,8]{0,1:T(8,128)}, f32[512,8,128]{2,0,1:T(8,128)S(1)})) conditional(s32[]{:T(128)} %convert_element_type.25, (f32[512,8]{0,1:T(8,128)S(1)}, f32[512,8]{0,1:T(8,128)}, f32[512,8,128]{2,0,1:T(8,128)S(1)}) %tuple.76, (s32[512]{0:T(512)}, s32[512]{0:T(512)}, s32[1024]{0:T(1024)}, s32[]{:T(128)}, ...), branch_computations={%region_4.4_spmd, %region_5.7_spmd.clone} | conditional | flops 1098922496 | bytes 33194124 | solution.py:78
  63.7 1.0 or_and_fusion
  64.8 1.5 %fusion.4 = (f32[512,8]{0,1:T(8,128)S(1)}, f32[512,512,8]{1,0,2:T(8,128)S(1)}) fusion(pred[512,512]{0,1:T(8,128)(4,1)S(1)} %or_and_fusion, bf16[512,8,128]{2,0,1:T(8,128)(2,1)S(1)} %get-tuple-element.552, bf16[1024,128]{1,0:T(8,128)(2,1)S(1)} %get-tuple-element.551, s32[]{:T(128)} %get-tuple-element.548), kind=kOutput, calls=%fused_computation.8 | convolution fusion | flops 543158272 | bytes 9846788 | tf_op jit(solution)/shard_map/while/body/eval_jaxpr/while/body/eval_jaxpr/cond/branch_1_fun/qhd,kd->qhk/dot_general | solution.py:25
  66.3 1.7 %fusion.3 = f32[512,8]{0,1:T(8,128)S(1)} fusion(f32[512,512,8]{1,0,2:T(8,128)S(1)} %get-tuple-element.622, f32[512,8]{0,1:T(8,128)S(1)} %max.5, pred[512,512]{0,1:T(8,128)(4,1)S(1)} %or_and_fusion), kind=kLoop, calls=%fused_computation.7 | loop fusion | flops 8384512 | bytes 8683520 | tf_op jit(solution)/shard_map/while/body/eval_jaxpr/while/body/eval_jaxpr/cond/branch_1_fun/reduce_sum | solution.py:35
  68.1 2.8 %multiply_add_fusion = f32[512,8,128]{2,0,1:T(8,128)S(1)} fusion(f32[512,8,128]{2,0,1:T(8,128)S(1)} %get-tuple-element.554, f32[512,512,8]{1,0,2:T(8,128)S(1)} %get-tuple-element.622, f32[512,8]{0,1:T(8,128)S(1)} %max.5, pred[512,512]{0,1:T(8,128)(4,1)S(1)} %or_and_fusion, f32[512,8]{0,1:T(8,128)S(1)} %get-tuple-element.618, ...), kind=kOutput, calls=%fused_computation.11 | convolution fusion | flops 546308096 | bytes 13008900 | tf_op jit(solution)/shard_map/while/body/eval_jaxpr/while/body/eval_jaxpr/cond/branch_1_fun/qhk,kd->qhd/dot_general | solution.py:36
  71.0 2.0 %fusion.67 = (s32[]{:T(128)}, s32[512]{0:T(512)}) fusion(s32[1024]{0:T(1024)} %get-tuple-element.768, s32[]{:T(128)} %select_n.391), kind=kLoop, calls=%fused_computation.117.clone.1 | loop fusion | flops 511 | bytes 4104 | tf_op jit(solution)/shard_map/while/body/eval_jaxpr/while/body/eval_jaxpr/reduce_min | solution.py:79
  77.3 9.5 %conditional.3 = ((f32[512,8]{0,1:T(8,128)S(1)}, f32[512,8]{0,1:T(8,128)}, f32[512,8,128]{2,0,1:T(8,128)S(1)})) conditional(s32[]{:T(128)} %convert_element_type.25, (f32[512,8]{0,1:T(8,128)S(1)}, f32[512,8]{0,1:T(8,128)}, f32[512,8,128]{2,0,1:T(8,128)S(1)}) %tuple.76, (s32[512]{0:T(512)}, s32[512]{0:T(512)}, s32[1024]{0:T(1024)}, s32[]{:T(128)}, ...), branch_computations={%region_4.4_spmd, %region_5.7_spmd.clone} | conditional | flops 1098922496 | bytes 33194124 | solution.py:78
  80.6 1.5 %fusion.4 = (f32[512,8]{0,1:T(8,128)S(1)}, f32[512,512,8]{1,0,2:T(8,128)S(1)}) fusion(pred[512,512]{0,1:T(8,128)(4,1)S(1)} %or_and_fusion, bf16[512,8,128]{2,0,1:T(8,128)(2,1)S(1)} %get-tuple-element.552, bf16[1024,128]{1,0:T(8,128)(2,1)S(1)} %get-tuple-element.551, s32[]{:T(128)} %get-tuple-element.548), kind=kOutput, calls=%fused_computation.8 | convolution fusion | flops 543158272 | bytes 9846788 | tf_op jit(solution)/shard_map/while/body/eval_jaxpr/while/body/eval_jaxpr/cond/branch_1_fun/qhd,kd->qhk/dot_general | solution.py:25
  82.1 1.7 %fusion.3 = f32[512,8]{0,1:T(8,128)S(1)} fusion(f32[512,512,8]{1,0,2:T(8,128)S(1)} %get-tuple-element.622, f32[512,8]{0,1:T(8,128)S(1)} %max.5, pred[512,512]{0,1:T(8,128)(4,1)S(1)} %or_and_fusion), kind=kLoop, calls=%fused_computation.7 | loop fusion | flops 8384512 | bytes 8683520 | tf_op jit(solution)/shard_map/while/body/eval_jaxpr/while/body/eval_jaxpr/cond/branch_1_fun/reduce_sum | solution.py:35
  83.9 2.8 %multiply_add_fusion = f32[512,8,128]{2,0,1:T(8,128)S(1)} fusion(f32[512,8,128]{2,0,1:T(8,128)S(1)} %get-tuple-element.554, f32[512,512,8]{1,0,2:T(8,128)S(1)} %get-tuple-element.622, f32[512,8]{0,1:T(8,128)S(1)} %max.5, pred[512,512]{0,1:T(8,128)(4,1)S(1)} %or_and_fusion, f32[512,8]{0,1:T(8,128)S(1)} %get-tuple-element.618, ...), kind=kOutput, calls=%fused_computation.11 | convolution fusion | flops 546308096 | bytes 13008900 | tf_op jit(solution)/shard_map/while/body/eval_jaxpr/while/body/eval_jaxpr/cond/branch_1_fun/qhk,kd->qhd/dot_general | solution.py:36
  86.8 1.9 %copy.37 = f32[512,8,128]{0,2,1:T(8,128)} copy(f32[512,8,128]{2,0,1:T(8,128)S(1)} %get-tuple-element.428) | data formatting | bytes 4194304 | tf_op jit(solution)/shard_map/while/body/eval_jaxpr/while | solution.py:96
  88.7 1.9 %divide_convert_fusion = bf16[512,8,128]{0,2,1:T(8,128)(2,1)S(1)} fusion(f32[512,8,128]{0,2,1:T(8,128)} %copy.37, f32[512,8]{0,1:T(8,128)} %get-tuple-element.429), kind=kLoop, calls=%fused_computation.36 | loop fusion | flops 1048576 | bytes 3162112 | tf_op jit(solution)/shard_map/convert_element_type | solution.py:181
  91.0 1.5 %reduce = bf16[512,1024]{0,1:T(8,128)(2,1)S(1)} reduce(bf16[512,1,1024]{0,2,1:T(8,128)(2,1)S(1)} %bitcast.67, bf16[]{:T(256)} %broadcast.462), dimensions={1}, to_apply=%copy.38.reduce_sub_computation | reduce | bytes 2097154 | tf_op jit(solution)/shard_map/reshape | solution.py:182
  93.8 29.9 %all_to_all.60 = bf16[8,2,32768]{2,1,0:T(2,128)(2,1)S(1)} all-to-all(bf16[8,2,32768]{2,1,0:T(2,128)(2,1)S(1)} %reshape.331), channel_id=1, replica_groups=mesh['groups'=2,'ulysses'=8,'seq'=2] {'ulysses'}, dimensions={0} | all-to-all | bytes 2097152 | tf_op jit(solution)/shard_map/all_to_all | solution.py:184
  123.7 1.0 reshape.332
  125.2 1.1 copy.46
  (58 shorter events, 17.8 us)
Async XLA Ops:
  0.0 0.9 copy-start
  0.0 36.2 %copy-start.1 = (s32[1024]{0:T(1024)S(1)}, s32[1024]{0:T(1024)}, u32[]{:S(2)}) copy-start(s32[1024]{0:T(1024)} %param.12) | copy-start | bytes 12292
  0.9 37.7 %copy-start.5 = (s32[128]{0:T(128)S(1)}, s32[128]{0:T(128)}, u32[]{:S(2)}) copy-start(s32[128]{0:T(128)} %param.13) | copy-start | bytes 1540
  1.6 14.6 %all-to-all-start = ((bf16[64,8,128]{2,0,1:T(8,128)(2,1)}), bf16[64,8,128]{2,0,1:T(8,128)(2,1)S(1)}, u32[]{:S(2)}, u32[]{:S(2)}) async-start(bf16[64,8,128]{2,0,1:T(8,128)(2,1)} %copy_bitcast_fusion.2), calls=%async_computation | async-start | bytes 262144 | tf_op jit(solution)/shard_map/all_to_all | solution.py:147
  16.2 10.7 %all-to-all-start.2 = ((bf16[64,8,128]{2,0,1:T(8,128)(2,1)}), bf16[64,8,128]{2,0,1:T(8,128)(2,1)S(1)}, u32[]{:S(2)}, u32[]{:S(2)}) async-start(bf16[64,8,128]{2,0,1:T(8,128)(2,1)} %copy_bitcast_fusion.1), calls=%async_computation.2 | async-start | bytes 262144 | tf_op jit(solution)/shard_map/all_to_all | solution.py:150
  26.9 27.2 %all-to-all-start.1 = ((bf16[64,8,1024]{2,0,1:T(8,128)(2,1)}), bf16[64,8,1024]{2,0,1:T(8,128)(2,1)S(1)}, u32[]{:S(2)}, u32[]{:S(2)}) async-start(bf16[64,8,1024]{2,0,1:T(8,128)(2,1)} %bitcast.66), calls=%async_computation.1 | async-start | bytes 2097152 | tf_op jit(solution)/shard_map/all_to_all | solution.py:127
  64.8 3.3 %copy-start.2 = (f32[512,8]{0,1:T(8,128)S(1)}, f32[512,8]{0,1:T(8,128)}, u32[]{:S(2)}) copy-start(f32[512,8]{0,1:T(8,128)} %get-tuple-element.553) | copy-start | bytes 49156 | tf_op jit(solution)/shard_map/while/body/eval_jaxpr/while/body/eval_jaxpr/cond
  64.8 3.3 %copy-start.4 = (bf16[1024,128]{1,0:T(8,128)(2,1)S(1)}, bf16[1024,128]{1,0:T(8,128)(2,1)}, u32[]{:S(2)}) copy-start(bf16[1024,128]{1,0:T(8,128)(2,1)} %get-tuple-element.555) | copy-start | bytes 786436 | tf_op jit(solution)/shard_map/while/body/eval_jaxpr/while/body/eval_jaxpr/cond
  68.1 2.9 %copy-start.3 = (f32[512,8]{0,1:T(8,128)}, f32[512,8]{0,1:T(8,128)S(1)}, u32[]{:S(2)}) copy-start(f32[512,8]{0,1:T(8,128)S(1)} %get-tuple-element.726) | copy-start | bytes 49156 | tf_op jit(solution)/shard_map/while/body/eval_jaxpr/while/body/eval_jaxpr/cond
  80.6 3.3 %copy-start.2 = (f32[512,8]{0,1:T(8,128)S(1)}, f32[512,8]{0,1:T(8,128)}, u32[]{:S(2)}) copy-start(f32[512,8]{0,1:T(8,128)} %get-tuple-element.553) | copy-start | bytes 49156 | tf_op jit(solution)/shard_map/while/body/eval_jaxpr/while/body/eval_jaxpr/cond
  80.6 3.3 %copy-start.4 = (bf16[1024,128]{1,0:T(8,128)(2,1)S(1)}, bf16[1024,128]{1,0:T(8,128)(2,1)}, u32[]{:S(2)}) copy-start(bf16[1024,128]{1,0:T(8,128)(2,1)} %get-tuple-element.555) | copy-start | bytes 786436 | tf_op jit(solution)/shard_map/while/body/eval_jaxpr/while/body/eval_jaxpr/cond
  83.9 2.9 %copy-start.3 = (f32[512,8]{0,1:T(8,128)}, f32[512,8]{0,1:T(8,128)S(1)}, u32[]{:S(2)}) copy-start(f32[512,8]{0,1:T(8,128)S(1)} %get-tuple-element.726) | copy-start | bytes 49156 | tf_op jit(solution)/shard_map/while/body/eval_jaxpr/while/body/eval_jaxpr/cond
where the time goes:
time: 127 us; the launch traced here: 126 us
  local copies, waits for them, and re-layouts  34.1 us (27%)
  blocking collectives  34 us (27%)
  other arithmetic  19.5 us (15%)
  starting transfers between devices  14.2 us (11%)
  waiting for transfers between devices  12.6 us (10%)
  matrix products  8.7 us (7%)
  loops' own time  2.94 us (2%)
    all_to_all x1, blocking collectives, shards(): lax.all_to_all(result, 'ulysses', split_axis=0, concat_axis=1, tiled=True)  29.9 us
    all_to_all x1, starting transfers between devices, shards(): lax.all_to_all(spread(key_states, ulysses_count), 'ulysses', split_axis=1...  7.28 us
    gather x1, local copies, waits for them, and re-layouts, shards(): jnp.take(judged, key_place)  6.8 us
    all_to_all x1, waiting for transfers between devices, shards(): lax.all_to_all(spread(key_states, ulysses_count), 'ulysses', split_axis=1...  5.76 us
    gather x1, local copies, waits for them, and re-layouts, shards(): jnp.take(turn_ids, key_place)  5.72 us
    dot_general x2, matrix products, absorb(): jnp.einsum('qhk,kd->qhd', weights.astype(jnp.bfloat16), values_block, pre...  5.69 us
    unnamed x13, local copies, waits for them, and re-layouts  5.12 us
    all_to_all x1, waiting for transfers between devices, shards(): lax.all_to_all(spread(value_states, ulysses_count), 'ulysses', split_axis...  4.99 us
  transfers between devices with their start and end apart: 3, of which 3 were waited for; matrix products, arithmetic and copies ran while one was open for 17% of the time, Pallas kernels for 0%

commit v1 on v0

--- a/solution.py
+++ b/solution.py
@@ -144,8 +144,16 @@
         jnp.zeros((query_total, heads_here, HEAD_DIM), jnp.float32),
     )
     keys_out, values_out = (
-        lax.all_to_all(
-            spread(key_states, ulysses_count), "ulysses", split_axis=1, concat_axis=0, tiled=True
+        jnp.concatenate(
+            lax.all_to_all(
+                jnp.stack(
+                    jnp.split(spread(key_states, ulysses_count), lax.axis_size("ulysses"), axis=1)
+                ),
+                "ulysses",
+                0,
+                0,
+            ),
+            axis=0,
         ),
         lax.all_to_all(
             spread(value_states, ulysses_count), "ulysses", split_axis=1, concat_axis=0, tiled=True

time: 127 us -> 130 us (1.024)
  local copies, waits for them, and re-layouts: 34.1 us -> 36.5 us
  waiting for transfers between devices: 12.6 us -> 14.8 us
    unnamed x13 -> x21, local copies, waits for them, and re-layouts: 5.12 us -> 9.44 us
    another operation x2 -> x1, local copies, waits for them, and re-layouts: 2.26 us -> 0.67 us  [spread(): return widened.reshape(row_count, copies, HEAD_DIM)]
  transfers between devices with their start and end apart: 3 -> 3, of which waited for: 3 -> 3; matrix products, arithmetic and copies ran while one was open for 17% -> 15% of each run, Pallas kernels for 0% -> 0%
where the time goes in v1:
time: 130 us; the launch traced here: 129 us
  local copies, waits for them, and re-layouts  36.5 us (28%)
  blocking collectives  32.8 us (25%)
  other arithmetic  19.2 us (15%)
  waiting for transfers between devices  14.8 us (11%)
  starting transfers between devices  14.2 us (11%)
  matrix products  8.7 us (7%)
  loops' own time  2.63 us (2%)
    all_to_all x1, blocking collectives, shards(): lax.all_to_all(result, 'ulysses', split_axis=0, concat_axis=1, tiled=True)  28.7 us
    unnamed x21, local copies, waits for them, and re-layouts  9.44 us
    all_to_all x1, starting transfers between devices, shards(): lax.all_to_all(jnp.stack(jnp.split(spread(key_states, ulysses_count), lax...  7.29 us
    gather x1, local copies, waits for them, and re-layouts, shards(): jnp.take(judged, key_place)  6.8 us
    all_to_all x1, waiting for transfers between devices, shards(): lax.all_to_all(jnp.stack(jnp.split(spread(key_states, ulysses_count), lax...  6.67 us
    dot_general x2, matrix products, absorb(): jnp.einsum('qhk,kd->qhd', weights.astype(jnp.bfloat16), values_block, pre...  5.68 us
    all_to_all x1, waiting for transfers between devices, shards(): lax.all_to_all(spread(value_states, ulysses_count), 'ulysses', split_axis...  4.99 us
    gather x1, local copies, waits for them, and re-layouts, shards(): jnp.take(turn_ids, key_place)  4.53 us
  transfers between devices with their start and end apart: 3, of which 3 were waited for; matrix products, arithmetic and copies ran while one was open for 15% of the time, Pallas kernels for 0%

profile of v1, /device:TPU:0, one launch (start us, length us, event | category | flops | bytes accessed | tf_op | source)
XLA Modules:
  0.0 129.1 jit_solution(7194257376772716173)
XLA Ops:
  6.1 7.3 %all-to-all-start = ((bf16[8,64,1,128]{3,1,2,0:T(8,128)(2,1)}), bf16[8,64,1,128]{3,1,2,0:T(8,128)(2,1)S(1)}, u32[]{:S(2)}, u32[]{:S(2)}) async-start(bf16[8,64,1,128]{3,1,2,0:T(8,128)(2,1)} %constant_dynamic-update-slice_fusion), calls=%async_computation | async-start | bytes 262144 | tf_op jit(solution)/shard_map/all_to_all | solution.py:148
  14.0 6.7 %all-to-all-done = bf16[8,64,1,128]{3,1,2,0:T(8,128)(2,1)S(1)} async-done(((bf16[8,64,1,128]{3,1,2,0:T(8,128)(2,1)}), bf16[8,64,1,128]{3,1,2,0:T(8,128)(2,1)S(1)}, u32[]{:S(2)}, u32[]{:S(2)}) %all-to-all-start) | async-done | bytes 131104 | tf_op jit(solution)/shard_map/all_to_all | solution.py:148
  20.7 3.4 %all-to-all-start.2 = ((bf16[64,8,128]{2,0,1:T(8,128)(2,1)}), bf16[64,8,128]{2,0,1:T(8,128)(2,1)S(1)}, u32[]{:S(2)}, u32[]{:S(2)}) async-start(bf16[64,8,128]{2,0,1:T(8,128)(2,1)} %copy_bitcast_fusion.1), calls=%async_computation.2 | async-start | bytes 262144 | tf_op jit(solution)/shard_map/all_to_all | solution.py:158
  24.1 2.3 %copy.176 = bf16[8,8,8,1024]{3,2,0,1:T(8,128)(2,1)} copy(bf16[8,8,8,1024]{3,2,1,0:T(8,128)(2,1)} %bitcast.81) | data formatting | bytes 2097152 | tf_op jit(solution)/shard_map/reshape | solution.py:128
  26.4 5.0 %all-to-all-done.2 = bf16[64,8,128]{2,0,1:T(8,128)(2,1)S(1)} async-done(((bf16[64,8,128]{2,0,1:T(8,128)(2,1)}), bf16[64,8,128]{2,0,1:T(8,128)(2,1)S(1)}, u32[]{:S(2)}, u32[]{:S(2)}) %all-to-all-start.2) | async-done | bytes 131104 | tf_op jit(solution)/shard_map/all_to_all | solution.py:158
  31.4 3.6 %all-to-all-start.1 = ((bf16[64,8,1024]{2,0,1:T(8,128)(2,1)}), bf16[64,8,1024]{2,0,1:T(8,128)(2,1)S(1)}, u32[]{:S(2)}, u32[]{:S(2)}) async-start(bf16[64,8,1024]{2,0,1:T(8,128)(2,1)} %bitcast.75), calls=%async_computation.1 | async-start | bytes 2097152 | tf_op jit(solution)/shard_map/all_to_all | solution.py:127
  35.0 4.5 %gather_fusion = s32[1024]{0:T(1024)S(1)} fusion(s32[1024]{0:T(1024)S(1)} %copy-done.1, s32[1024]{0:T(1024)S(1)} %broadcast_clamp_fusion), kind=kCustom, calls=%fused_computation | custom fusion | bytes 12288 | tf_op jit(solution)/shard_map/jit(_take)/gather | solution.py:183
  39.6 2.3 %gather_fusion.1 = s32[512]{0:T(512)S(1)} fusion(s32[1024]{0:T(1024)S(1)} %copy-done.1, s32[1024]{0:T(1024)S(1)} %pad_clamp_fusion), kind=kCustom, calls=%fused_computation.1 | custom fusion | bytes 6144 | tf_op jit(solution)/shard_map/jit(_take)/gather | solution.py:140
  42.1 6.8 %gather_fusion.2 = pred[1024]{0:T(1024)(128)(4,1)S(1)} fusion(pred[1024]{0:T(1024)(128)(4,1)S(1)} %fusion.24, s32[1024]{0:T(1024)S(1)} %broadcast_clamp_fusion), kind=kCustom, calls=%fused_computation.2 | custom fusion | bytes 6144 | tf_op jit(solution)/shard_map/jit(_take)/gather | solution.py:184
  49.5 1.2 and_select_fusion.6
  51.3 2.0 %all_gather.6 = bf16[1024,128]{1,0:T(8,128)(2,1)S(1)} all-gather(bf16[512,128]{1,0:T(8,128)(2,1)S(1)} %bitcast.82), channel_id=1, replica_groups=mesh['groups'=2,'ulysses'=8,'seq'=2] {'seq'}, dimensions={0}, use_global_device_ids=true | all-gather | bytes 393216 | tf_op jit(solution)/shard_map/all_gather | solution.py:165
  53.3 2.1 %all_gather.7 = bf16[1024,128]{1,0:T(8,128)(2,1)} all-gather(bf16[512,128]{1,0:T(8,128)(2,1)S(1)} %bitcast.83), channel_id=1, replica_groups=mesh['groups'=2,'ulysses'=8,'seq'=2] {'seq'}, dimensions={0}, use_global_device_ids=true | all-gather | bytes 393216 | tf_op jit(solution)/shard_map/all_gather | solution.py:166
  55.4 3.2 %all-to-all-done.1 = bf16[64,8,1024]{2,0,1:T(8,128)(2,1)S(1)} async-done(((bf16[64,8,1024]{2,0,1:T(8,128)(2,1)}), bf16[64,8,1024]{2,0,1:T(8,128)(2,1)S(1)}, u32[]{:S(2)}, u32[]{:S(2)}) %all-to-all-start.1) | async-done | bytes 1048608 | tf_op jit(solution)/shard_map/all_to_all | solution.py:127
  59.7 31.1 %while.31 = (s32[]{:T(128)}, f32[512,8]{0,1:T(8,128)S(1)}, f32[512,8]{0,1:T(8,128)}, f32[512,8,128]{2,0,1:T(8,128)S(1)}, s32[1024]{0:T(1024)}, /*index=5*/s32[]{...) while((s32[]{:T(128)}, f32[512,8]{0,1:T(8,128)S(1)}, ...), condition=%wide.region_8.9_spmd.clone, body=%wide.region_2.8_spmd.clone.sunk | while | flops 1098925056 | bytes 33209420 | solution.py:96
  59.7 2.0 %fusion.67 = (s32[]{:T(128)}, s32[512]{0:T(512)}) fusion(s32[1024]{0:T(1024)} %get-tuple-element.893, s32[]{:T(128)} %select_n.391), kind=kLoop, calls=%fused_computation.124.clone.1 | loop fusion | flops 511 | bytes 4104 | tf_op jit(solution)/shard_map/while/body/eval_jaxpr/while/body/eval_jaxpr/reduce_min | solution.py:79
  65.7 9.5 %conditional.3 = ((f32[512,8]{0,1:T(8,128)S(1)}, f32[512,8]{0,1:T(8,128)}, f32[512,8,128]{2,0,1:T(8,128)S(1)})) conditional(s32[]{:T(128)} %convert_element_type.25, (f32[512,8]{0,1:T(8,128)S(1)}, f32[512,8]{0,1:T(8,128)}, f32[512,8,128]{2,0,1:T(8,128)S(1)}) %tuple.92, (s32[512]{0:T(512)}, s32[512]{0:T(512)}, s32[1024]{0:T(1024)}, s32[]{:T(128)}, ...), branch_computations={%region_4.4_spmd, %region_5.7_spmd.clone} | conditional | flops 1098922496 | bytes 33194124 | solution.py:78
  68.0 1.0 or_and_fusion
  69.1 1.5 %fusion.4 = (f32[512,8]{0,1:T(8,128)S(1)}, f32[512,512,8]{1,0,2:T(8,128)S(1)}) fusion(pred[512,512]{0,1:T(8,128)(4,1)S(1)} %or_and_fusion, bf16[512,8,128]{2,0,1:T(8,128)(2,1)S(1)} %get-tuple-element.669, bf16[1024,128]{1,0:T(8,128)(2,1)S(1)} %get-tuple-element.668, s32[]{:T(128)} %get-tuple-element.665), kind=kOutput, calls=%fused_computation.8 | convolution fusion | flops 543158272 | bytes 9846788 | tf_op jit(solution)/shard_map/while/body/eval_jaxpr/while/body/eval_jaxpr/cond/branch_1_fun/qhd,kd->qhk/dot_general | solution.py:25
  70.6 1.7 %fusion.3 = f32[512,8]{0,1:T(8,128)S(1)} fusion(f32[512,512,8]{1,0,2:T(8,128)S(1)} %get-tuple-element.739, f32[512,8]{0,1:T(8,128)S(1)} %max.5, pred[512,512]{0,1:T(8,128)(4,1)S(1)} %or_and_fusion), kind=kLoop, calls=%fused_computation.7 | loop fusion | flops 8384512 | bytes 8683520 | tf_op jit(solution)/shard_map/while/body/eval_jaxpr/while/body/eval_jaxpr/cond/branch_1_fun/reduce_sum | solution.py:35
  72.4 2.8 %multiply_add_fusion = f32[512,8,128]{2,0,1:T(8,128)S(1)} fusion(f32[512,8,128]{2,0,1:T(8,128)S(1)} %get-tuple-element.671, f32[512,512,8]{1,0,2:T(8,128)S(1)} %get-tuple-element.739, f32[512,8]{0,1:T(8,128)S(1)} %max.5, pred[512,512]{0,1:T(8,128)(4,1)S(1)} %or_and_fusion, f32[512,8]{0,1:T(8,128)S(1)} %get-tuple-element.735, ...), kind=kOutput, calls=%fused_computation.11 | convolution fusion | flops 546308096 | bytes 13008900 | tf_op jit(solution)/shard_map/while/body/eval_jaxpr/while/body/eval_jaxpr/cond/branch_1_fun/qhk,kd->qhd/dot_general | solution.py:36
  75.3 2.0 %fusion.67 = (s32[]{:T(128)}, s32[512]{0:T(512)}) fusion(s32[1024]{0:T(1024)} %get-tuple-element.893, s32[]{:T(128)} %select_n.391), kind=kLoop, calls=%fused_computation.124.clone.1 | loop fusion | flops 511 | bytes 4104 | tf_op jit(solution)/shard_map/while/body/eval_jaxpr/while/body/eval_jaxpr/reduce_min | solution.py:79
  81.3 9.5 %conditional.3 = ((f32[512,8]{0,1:T(8,128)S(1)}, f32[512,8]{0,1:T(8,128)}, f32[512,8,128]{2,0,1:T(8,128)S(1)})) conditional(s32[]{:T(128)} %convert_element_type.25, (f32[512,8]{0,1:T(8,128)S(1)}, f32[512,8]{0,1:T(8,128)}, f32[512,8,128]{2,0,1:T(8,128)S(1)}) %tuple.92, (s32[512]{0:T(512)}, s32[512]{0:T(512)}, s32[1024]{0:T(1024)}, s32[]{:T(128)}, ...), branch_computations={%region_4.4_spmd, %region_5.7_spmd.clone} | conditional | flops 1098922496 | bytes 33194124 | solution.py:78
  83.6 1.0 or_and_fusion
  84.6 1.5 %fusion.4 = (f32[512,8]{0,1:T(8,128)S(1)}, f32[512,512,8]{1,0,2:T(8,128)S(1)}) fusion(pred[512,512]{0,1:T(8,128)(4,1)S(1)} %or_and_fusion, bf16[512,8,128]{2,0,1:T(8,128)(2,1)S(1)} %get-tuple-element.669, bf16[1024,128]{1,0:T(8,128)(2,1)S(1)} %get-tuple-element.668, s32[]{:T(128)} %get-tuple-element.665), kind=kOutput, calls=%fused_computation.8 | convolution fusion | flops 543158272 | bytes 9846788 | tf_op jit(solution)/shard_map/while/body/eval_jaxpr/while/body/eval_jaxpr/cond/branch_1_fun/qhd,kd->qhk/dot_general | solution.py:25
  86.1 1.7 %fusion.3 = f32[512,8]{0,1:T(8,128)S(1)} fusion(f32[512,512,8]{1,0,2:T(8,128)S(1)} %get-tuple-element.739, f32[512,8]{0,1:T(8,128)S(1)} %max.5, pred[512,512]{0,1:T(8,128)(4,1)S(1)} %or_and_fusion), kind=kLoop, calls=%fused_computation.7 | loop fusion | flops 8384512 | bytes 8683520 | tf_op jit(solution)/shard_map/while/body/eval_jaxpr/while/body/eval_jaxpr/cond/branch_1_fun/reduce_sum | solution.py:35
  87.9 2.8 %multiply_add_fusion = f32[512,8,128]{2,0,1:T(8,128)S(1)} fusion(f32[512,8,128]{2,0,1:T(8,128)S(1)} %get-tuple-element.671, f32[512,512,8]{1,0,2:T(8,128)S(1)} %get-tuple-element.739, f32[512,8]{0,1:T(8,128)S(1)} %max.5, pred[512,512]{0,1:T(8,128)(4,1)S(1)} %or_and_fusion, f32[512,8]{0,1:T(8,128)S(1)} %get-tuple-element.735, ...), kind=kOutput, calls=%fused_computation.11 | convolution fusion | flops 546308096 | bytes 13008900 | tf_op jit(solution)/shard_map/while/body/eval_jaxpr/while/body/eval_jaxpr/cond/branch_1_fun/qhk,kd->qhd/dot_general | solution.py:36
  90.8 1.9 %copy.147 = f32[512,8,128]{0,2,1:T(8,128)} copy(f32[512,8,128]{2,0,1:T(8,128)S(1)} %get-tuple-element.428) | data formatting | bytes 4194304 | tf_op jit(solution)/shard_map/while/body/eval_jaxpr/while | solution.py:96
  92.7 1.9 %divide_convert_fusion = bf16[512,8,128]{0,2,1:T(8,128)(2,1)S(1)} fusion(f32[512,8,128]{0,2,1:T(8,128)} %copy.147, f32[512,8]{0,1:T(8,128)} %get-tuple-element.429), kind=kLoop, calls=%fused_computation.36 | loop fusion | flops 1048576 | bytes 3162112 | tf_op jit(solution)/shard_map/convert_element_type | solution.py:189
  95.1 1.5 %reduce = bf16[512,1024]{0,1:T(8,128)(2,1)S(1)} reduce(bf16[512,1,1024]{0,2,1:T(8,128)(2,1)S(1)} %bitcast.76, bf16[]{:T(256)} %broadcast.462), dimensions={1}, to_apply=%copy.148.reduce_sub_computation | reduce | bytes 2097154 | tf_op jit(solution)/shard_map/reshape | solution.py:190
  97.9 28.7 %all_to_all.50 = bf16[8,2,32768]{2,1,0:T(2,128)(2,1)S(1)} all-to-all(bf16[8,2,32768]{2,1,0:T(2,128)(2,1)S(1)} %reshape.326), channel_id=1, replica_groups=mesh['groups'=2,'ulysses'=8,'seq'=2] {'ulysses'}, dimensions={0} | all-to-all | bytes 2097152 | tf_op jit(solution)/shard_map/all_to_all | solution.py:192
  126.6 1.0 reshape.327
  128.0 1.1 copy.164
  (67 shorter events, 21.9 us)
Async XLA Ops:
  0.0 13.4 %copy-start = (bf16[64,1024]{1,0:T(8,128)(2,1)S(1)}, bf16[64,1024]{1,0:T(8,128)(2,1)}, u32[]{:S(2)}) copy-start(bf16[64,1024]{1,0:T(8,128)(2,1)} %param.11) | copy-start | bytes 393220
  0.0 35.0 %copy-start.1 = (s32[1024]{0:T(1024)S(1)}, s32[1024]{0:T(1024)}, u32[]{:S(2)}) copy-start(s32[1024]{0:T(1024)} %param.12) | copy-start | bytes 12292
  0.0 41.9 %copy-start.5 = (s32[128]{0:T(128)S(1)}, s32[128]{0:T(128)}, u32[]{:S(2)}) copy-start(s32[128]{0:T(128)} %param.13) | copy-start | bytes 1540
  6.1 14.6 %all-to-all-start = ((bf16[8,64,1,128]{3,1,2,0:T(8,128)(2,1)}), bf16[8,64,1,128]{3,1,2,0:T(8,128)(2,1)S(1)}, u32[]{:S(2)}, u32[]{:S(2)}) async-start(bf16[8,64,1,128]{3,1,2,0:T(8,128)(2,1)} %constant_dynamic-update-slice_fusion), calls=%async_computation | async-start | bytes 262144 | tf_op jit(solution)/shard_map/all_to_all | solution.py:148
  20.7 10.7 %all-to-all-start.2 = ((bf16[64,8,128]{2,0,1:T(8,128)(2,1)}), bf16[64,8,128]{2,0,1:T(8,128)(2,1)S(1)}, u32[]{:S(2)}, u32[]{:S(2)}) async-start(bf16[64,8,128]{2,0,1:T(8,128)(2,1)} %copy_bitcast_fusion.1), calls=%async_computation.2 | async-start | bytes 262144 | tf_op jit(solution)/shard_map/all_to_all | solution.py:158
  31.4 27.2 %all-to-all-start.1 = ((bf16[64,8,1024]{2,0,1:T(8,128)(2,1)}), bf16[64,8,1024]{2,0,1:T(8,128)(2,1)S(1)}, u32[]{:S(2)}, u32[]{:S(2)}) async-start(bf16[64,8,1024]{2,0,1:T(8,128)(2,1)} %bitcast.75), calls=%async_computation.1 | async-start | bytes 2097152 | tf_op jit(solution)/shard_map/all_to_all | solution.py:127
  69.0 3.3 %copy-start.2 = (f32[512,8]{0,1:T(8,128)S(1)}, f32[512,8]{0,1:T(8,128)}, u32[]{:S(2)}) copy-start(f32[512,8]{0,1:T(8,128)} %get-tuple-element.670) | copy-start | bytes 49156 | tf_op jit(solution)/shard_map/while/body/eval_jaxpr/while/body/eval_jaxpr/cond
  69.0 3.3 %copy-start.4 = (bf16[1024,128]{1,0:T(8,128)(2,1)S(1)}, bf16[1024,128]{1,0:T(8,128)(2,1)}, u32[]{:S(2)}) copy-start(bf16[1024,128]{1,0:T(8,128)(2,1)} %get-tuple-element.672) | copy-start | bytes 786436 | tf_op jit(solution)/shard_map/while/body/eval_jaxpr/while/body/eval_jaxpr/cond
  72.4 2.9 %copy-start.3 = (f32[512,8]{0,1:T(8,128)}, f32[512,8]{0,1:T(8,128)S(1)}, u32[]{:S(2)}) copy-start(f32[512,8]{0,1:T(8,128)S(1)} %get-tuple-element.851) | copy-start | bytes 49156 | tf_op jit(solution)/shard_map/while/body/eval_jaxpr/while/body/eval_jaxpr/cond
  84.6 3.3 %copy-start.2 = (f32[512,8]{0,1:T(8,128)S(1)}, f32[512,8]{0,1:T(8,128)}, u32[]{:S(2)}) copy-start(f32[512,8]{0,1:T(8,128)} %get-tuple-element.670) | copy-start | bytes 49156 | tf_op jit(solution)/shard_map/while/body/eval_jaxpr/while/body/eval_jaxpr/cond
  84.6 3.3 %copy-start.4 = (bf16[1024,128]{1,0:T(8,128)(2,1)S(1)}, bf16[1024,128]{1,0:T(8,128)(2,1)}, u32[]{:S(2)}) copy-start(bf16[1024,128]{1,0:T(8,128)(2,1)} %get-tuple-element.672) | copy-start | bytes 786436 | tf_op jit(solution)/shard_map/while/body/eval_jaxpr/while/body/eval_jaxpr/cond
  87.9 2.9 %copy-start.3 = (f32[512,8]{0,1:T(8,128)}, f32[512,8]{0,1:T(8,128)S(1)}, u32[]{:S(2)}) copy-start(f32[512,8]{0,1:T(8,128)S(1)} %get-tuple-element.851) | copy-start | bytes 49156 | tf_op jit(solution)/shard_map/while/body/eval_jaxpr/while/body/eval_jaxpr/cond
